TPU v7x, 512 devices: a whole 4x4x16 slice. The times are simulated.
512 devices in a mesh: node: 64 (over y, z), local: 8 (over x, core).
Axes of the slice: x: 4, y: 4, z: 16, core: 2. Of those that a mesh axis runs over, the one named last changes fastest.
Arguments:
- grad_out: bfloat16 [65536, 3584], P(('node', 'local')), may hold values from -6 to 6
- expert_ids: int32 [65536, 8], P(('node', 'local')), may hold values from 0 to 255, as said below
- gate_weights: float32 [65536, 8], P(('node', 'local')), may hold values from 0.05 to 0.35
- saved_hidden: bfloat16 [64, 1024, 1024], P('node', None, 'local'), may hold values from -0.59765625 to 0.59765625
- down_weight: bfloat16 [64, 1024, 3584], P('node', 'local'), may hold values from -0.1875 to 0.1875
- second_moment: bfloat16 [64, 1024, 3584], P('node', 'local'), may hold values from 0.0019989014 to 0.25
Outputs:
- gate_weight_gradient: float32 [65536, 8], P(('node', 'local'))
- hidden_grad: bfloat16 [64, 1024, 1024], P('node', None, 'local')
- new_weight: bfloat16 [64, 1024, 3584], P('node', 'local')
- new_second: bfloat16 [64, 1024, 3584], P('node', 'local')
Inputs may be any that keep to these rules, and one draw needn't show every extreme that they name: `expert_ids`: each row names 8 different experts on at most 4 nodes (node = id // 4), two on each; at most one per row is in flight (id % 4 == 0). Among the rows of one device at most 2 name the in-flight expert of any one node, and in every draw some node receives exactly 2 from every device.
All inputs are finite; a program needn't handle non-finite values.
Results may differ from a plain program's by a relative error of at most 0.0051.
Values may be sent and summed in bfloat16 or wider, within the bound.
No kernel may reach another device: no remote copies, remote signals or barrier semaphores. Data moves between devices by JAX's collectives and lax.ppermute only.
A program may use at most 128 MiB of HBM per device.

v0:
```python
import jax
import jax.numpy as jnp
from jax import lax
from jax.sharding import PartitionSpec as P

EXPERTS_PER_HOST = 4
CAP = 2
beta_second = 0.95
learn_rate = 0.002
decay_rate = 0.1
epsilon = 1e-08
correct_second = 0.994079470779666


def gather_rows(picked_experts, gate_values, grads, node_count):
    transit_rows = picked_experts % EXPERTS_PER_HOST == 0
    row_present = jnp.any(transit_rows, 1)
    destination_node = jnp.sum(jnp.where(transit_rows, picked_experts // EXPERTS_PER_HOST, 0), 1)
    onehot = (
        (destination_node[:, None] == jnp.arange(node_count, dtype=jnp.int32)[None, :])
        & row_present[:, None]
    ).astype(jnp.int32)
    within_rank = jnp.sum(onehot * (jnp.cumsum(onehot, 0) - 1), 1)
    slot_index = destination_node * CAP + within_rank
    expert_location = (
        jnp.arange(node_count * CAP, dtype=jnp.int32)[:, None] == slot_index[None, :]
    ) & row_present[None, :]
    matched_gate = jnp.sum(jnp.where(transit_rows, gate_values, 0.0), 1).astype(jnp.bfloat16)
    departing_rows = jnp.dot(
        expert_location.astype(jnp.bfloat16), grads, preferred_element_type=jnp.float32
    ).astype(jnp.bfloat16)
    departing_gates = jnp.sum(
        jnp.where(expert_location, matched_gate.astype(jnp.float32)[None, :], 0.0), 1
    ).astype(jnp.bfloat16)
    feature_count = grads.shape[1]
    return (
        departing_rows.reshape(node_count, CAP, feature_count),
        departing_gates.reshape(node_count, CAP),
        expert_location,
        transit_rows,
    )


def on_device(grad_out, expert_ids, gate_weights, saved_hidden, down_weight, second_moment):
    node_count = lax.axis_size("node")
    members = lax.axis_size("local")
    feature_count = grad_out.shape[1]
    departing_rows, departing_gates, expert_location, transit_rows = gather_rows(
        expert_ids, gate_weights, grad_out, node_count
    )
    copies, copy_gates = (
        lax.all_gather(departing_rows[None], "local", axis=0, tiled=True),
        lax.all_gather(departing_gates[None], "local", axis=0, tiled=True),
    )
    arrived, arrived_gates = (
        lax.all_to_all(copies, "node", split_axis=1, concat_axis=1, tiled=True),
        lax.all_to_all(copy_gates, "node", split_axis=1, concat_axis=1, tiled=True),
    )
    arrived_rows = arrived.reshape(-1, feature_count)
    slot_gates = arrived_gates.reshape(-1).astype(jnp.float32)
    weight_now = down_weight[0]
    hidden_now = saved_hidden[0]
    unscaled = lax.dot_general(
        arrived_rows, weight_now, (((1,), (1,)), ((), ())), preferred_element_type=jnp.float32
    )
    hidden_out = (slot_gates[:, None] * unscaled).astype(jnp.bfloat16)
    slot_score = jnp.sum(unscaled * hidden_now.astype(jnp.float32), 1)
    scaled = (slot_gates[:, None] * arrived_rows.astype(jnp.float32)).astype(jnp.bfloat16)
    grad = lax.dot_general(
        hidden_now, scaled, (((0,), (0,)), ((), ())), preferred_element_type=jnp.float32
    )
    second_new = (
        beta_second * second_moment[0].astype(jnp.float32) + (1.0 - beta_second) * grad * grad
    )
    weight_f = weight_now.astype(jnp.float32)
    update = grad / (jnp.sqrt(second_new / correct_second) + epsilon) + decay_rate * weight_f
    weight_new = weight_f - learn_rate * update
    score_terms = slot_score.reshape(members, node_count * CAP)
    summed = lax.psum(score_terms, "local")
    own_terms = lax.dynamic_slice_in_dim(summed, lax.axis_index("local"), 1, 0)
    returned = lax.all_to_all(
        own_terms.reshape(node_count, CAP), "node", split_axis=0, concat_axis=0, tiled=True
    )
    returned_flat = returned.reshape(node_count * CAP)
    token_gradient = jnp.sum(jnp.where(expert_location, returned_flat[:, None], 0.0), 0)
    gate_weight_gradient = jnp.where(transit_rows, token_gradient[:, None], 0.0)
    return (
        gate_weight_gradient,
        hidden_out[None],
        weight_new.astype(jnp.bfloat16)[None],
        second_new.astype(jnp.bfloat16)[None],
    )


def solution(mesh):
    return jax.shard_map(
        on_device,
        mesh=mesh,
        in_specs=(
            P(("node", "local"), None),
            P(("node", "local"), None),
            P(("node", "local"), None),
            P("node", None, "local"),
            P("node", "local", None),
            P("node", "local", None),
        ),
        out_specs=(
            P(("node", "local"), None),
            P("node", None, "local"),
            P("node", "local", None),
            P("node", "local", None),
        ),
        check_vma=False,
    )
```

profile of v0, /device:TPU:2, one launch (start us, length us, event | category | flops | bytes accessed | tf_op | source)
XLA Modules:
  0.0 566.0 jit_solution(3273625820910826075)
XLA Ops:
  7.2 0.0 copy-start
  7.2 0.0 all-gather.2.cloned.1.call-start
  7.2 0.8 fusion.22
  8.0 0.7 fusion.19
  8.7 0.1 fusion.14
  8.8 0.2 reduce_window_sum.11
  9.0 0.2 select_reduce_fusion.2
  9.2 0.4 convolution_convert_fusion
  9.6 0.3 broadcast_in_dim_reshape.2
  9.9 1.0 copy.65
  11.0 0.0 all-gather.2.cloned.1.call-update
  11.0 56.7 %all-gather.2.cloned.1.call-done = bf16[8,64,2,3584]{3,1,2,0:T(8,128)(2,1)} async-done(((bf16[1,64,2,3584]{3,1,2,0:T(8,128)(2,1)}), bf16[8,64,2,3584]{3,1,2,0:T(8,128)(2,1)}) %all-gather.2.cloned.1.call-update) | async-done | bytes 7340048 | tf_op jit(solution)/shard_map/all_gather | solution.py:52
  67.7 14.7 %copy.66 = bf16[8,64,2,3584]{3,2,0,1:T(2,128)(2,1)} copy(bf16[8,64,2,3584]{3,1,2,0:T(8,128)(2,1)} %all-gather.2.cloned.1.call-done) | data formatting | bytes 14680064 | tf_op jit(solution)/shard_map/all_gather | solution.py:52
  82.4 16.0 %all-to-all-start = ((bf16[8,64,2,3584]{3,2,0,1:T(2,128)(2,1)}), bf16[8,64,2,3584]{3,2,0,1:T(2,128)(2,1)}, u32[]{:S(2)}, u32[]{:S(2)}) async-start(bf16[8,64,2,3584]{3,2,0,1:T(2,128)(2,1)} %copy.66), calls=%async_computation | async-start | bytes 14680064 | tf_op jit(solution)/shard_map/all_to_all | solution.py:56
  98.4 0.1 copy.69
  98.6 323.8 %all-to-all-done = bf16[8,64,2,3584]{3,2,0,1:T(2,128)(2,1)} async-done(((bf16[8,64,2,3584]{3,2,0,1:T(2,128)(2,1)}), bf16[8,64,2,3584]{3,2,0,1:T(2,128)(2,1)}, u32[]{:S(2)}, u32[]{:S(2)}) %all-to-all-start) | async-done | bytes 7340064 | tf_op jit(solution)/shard_map/all_to_all | solution.py:56
  422.4 7.4 %copy.67 = bf16[8,64,2,3584]{3,2,1,0:T(2,128)(2,1)} copy(bf16[8,64,2,3584]{3,2,0,1:T(2,128)(2,1)} %all-to-all-done) | data formatting | bytes 14680064 | tf_op jit(solution)/shard_map/all_to_all | solution.py:56
  429.8 15.5 %reshape.62 = bf16[1024,3584]{1,0:T(8,128)(2,1)} reshape(bf16[8,64,2,3584]{3,2,1,0:T(2,128)(2,1)} %copy.67) | data formatting | bytes 14680064 | tf_op jit(solution)/shard_map/reshape | solution.py:59
  445.4 5.6 multiply_reduce_fusion
  451.0 10.5 %psum.7 = f32[8,128]{1,0:T(8,128)S(1)} all-reduce(f32[8,128]{1,0:T(8,128)S(1)} %bitcast.41), channel_id=1, replica_groups=mesh['node'=64,'local'=8] {'local'}, use_global_device_ids=true, to_apply=%region_5.6 | all-reduce | flops 1024 | bytes 8192 | tf_op jit(solution)/shard_map/psum | solution.py:79
  461.5 0.8 all_to_all.13
  462.2 7.0 %all-to-all-start.1 = ((f32[64,1,2]{2,1,0:T(1,128)}), f32[64,1,2]{2,1,0:T(1,128)}, u32[]{:S(2)}, u32[]{:S(2)}) async-start(f32[64,1,2]{2,1,0:T(1,128)} %bitcast.3), calls=%async_computation.1 | async-start | bytes 65536 | tf_op jit(solution)/shard_map/all_to_all | solution.py:81
  469.2 0.5 select_reduce_fusion.3
  469.8 0.6 copy.68
  470.4 0.7 convert_element_type.132
  471.1 0.6 copy.78
  471.7 11.6 %all-to-all-done.1 = f32[64,1,2]{2,1,0:T(1,128)} async-done(((f32[64,1,2]{2,1,0:T(1,128)}), f32[64,1,2]{2,1,0:T(1,128)}, u32[]{:S(2)}, u32[]{:S(2)}) %all-to-all-start.1) | async-done | bytes 544 | tf_op jit(solution)/shard_map/all_to_all | solution.py:81
  483.3 0.5 broadcast.47
  483.8 1.5 reduce.7
  485.3 0.1 broadcast_in_dim.59
  485.4 0.1 select_reduce_fusion
  485.6 0.2 convert_element_type.82
  485.7 0.1 copy.71
  485.8 11.1 %all_gather.7 = bf16[8,64,2]{1,2,0:T(2,128)(2,1)S(1)} all-gather(bf16[1,64,2]{1,2,0:T(2,128)(2,1)S(1)} %copy.71), channel_id=1, replica_groups=mesh['node'=64,'local'=8] {'local'}, dimensions={0}, use_global_device_ids=true | all-gather | bytes 2304 | tf_op jit(solution)/shard_map/all_gather | solution.py:53
  496.9 0.7 copy.72
  497.6 4.8 all-to-all-start.2
  502.4 0.6 broadcast_select_fusion
  503.0 13.6 %all-to-all-done.2 = bf16[8,64,2]{0,2,1:T(2,128)(2,1)S(1)} async-done(((bf16[8,64,2]{0,2,1:T(2,128)(2,1)}), bf16[8,64,2]{0,2,1:T(2,128)(2,1)S(1)}, u32[]{:S(2)}, u32[]{:S(2)}) %all-to-all-start.2) | async-done | bytes 2080 | tf_op jit(solution)/shard_map/all_to_all | solution.py:57
  516.6 0.1 copy.73
  516.7 0.2 copy.74
  516.8 7.8 %multiply_convert_fusion = bf16[8,64,2,3584]{3,1,2,0:T(8,128)(2,1)S(1)} fusion(bf16[8,64,2,3584]{3,2,0,1:T(2,128)(2,1)} %all-to-all-done, f32[8,64,2]{1,2,0:T(2,128)S(1)} %copy.75), kind=kLoop, calls=%fused_computation | loop fusion | flops 11010048 | bytes 14684160 | tf_op jit(solution)/shard_map/convert_element_type | solution.py:68
  524.6 7.1 %copy.77 = bf16[8,64,2,3584]{3,2,1,0:T(2,128)(2,1)} copy(bf16[8,64,2,3584]{3,1,2,0:T(8,128)(2,1)S(1)} %multiply_convert_fusion) | data formatting | bytes 14680064 | tf_op jit(solution)/shard_map/convert_element_type | solution.py:68
  531.7 15.4 %convert_element_type.90 = bf16[1024,3584]{1,0:T(8,128)(2,1)} reshape(bf16[8,64,2,3584]{3,2,1,0:T(2,128)(2,1)} %copy.77) | data formatting | bytes 14680064 | tf_op jit(solution)/shard_map/convert_element_type | solution.py:68
  547.1 7.3 %fusion.5 = (bf16[1,128,3584]{1,2,0:T(8,128)(2,1)}, bf16[1,128,3584]{1,2,0:T(8,128)(2,1)}) fusion(bf16[1,128,3584]{1,2,0:T(8,128)(2,1)S(1)} %copy.78, bf16[1,128,3584]{1,2,0:T(8,128)(2,1)S(1)} %copy.68, bf16[1024,3584]{1,0:T(8,128)(2,1)} %convert_element_type.90, bf16[1,1024,128]{2,1,0:T(8,128)(2,1)S(1)} %copy-done.5), kind=kOutput, calls=%fused_computation.11 | convolution fusion | flops 946405376 | bytes 11272192 | tf_op jit(solution)/shard_map/dot_general | solution.py:69
  554.5 2.3 copy.80
  556.8 1.3 copy.81
  558.1 0.2 reshape.64
  558.3 0.8 copy.79
  (17 shorter events, 0.1 us)
Async XLA Ops:
  7.2 2.0 copy-start
  7.2 60.5 %all-gather.2.cloned.1.call-start = ((), (), s32[]{:S(2)}) async-start(), calls=%async_computation.3 | async-start | bytes 8257536 | tf_op jit(solution)/shard_map/all_gather | solution.py:52
  82.4 16.0 %copy-start.5 = (bf16[1,1024,128]{2,1,0:T(8,128)(2,1)S(1)}, bf16[1,1024,128]{2,1,0:T(8,128)(2,1)}, u32[]{:S(2)}) copy-start(bf16[1,1024,128]{2,1,0:T(8,128)(2,1)} %param.9) | copy-start | bytes 786436
  82.4 340.0 %all-to-all-start = ((bf16[8,64,2,3584]{3,2,0,1:T(2,128)(2,1)}), bf16[8,64,2,3584]{3,2,0,1:T(2,128)(2,1)}, u32[]{:S(2)}, u32[]{:S(2)}) async-start(bf16[8,64,2,3584]{3,2,0,1:T(2,128)(2,1)} %copy.66), calls=%async_computation | async-start | bytes 14680064 | tf_op jit(solution)/shard_map/all_to_all | solution.py:56
  429.8 15.5 %copy-start.2 = (bf16[1,128,3584]{2,1,0:T(8,128)(2,1)S(1)}, bf16[1,128,3584]{2,1,0:T(8,128)(2,1)}, u32[]{:S(2)}) copy-start(bf16[1,128,3584]{2,1,0:T(8,128)(2,1)} %param.10) | copy-start | bytes 2752516
  445.4 23.9 %copy-start.6 = (f32[128,8]{0,1:T(8,128)S(1)}, f32[128,8]{0,1:T(8,128)}, u32[]{:S(2)}) copy-start(f32[128,8]{0,1:T(8,128)} %param.8) | copy-start | bytes 12292
  450.9 20.1 %copy-start.3 = (bf16[1,128,3584]{2,1,0:T(8,128)(2,1)S(1)}, bf16[1,128,3584]{2,1,0:T(8,128)(2,1)}, u32[]{:S(2)}) copy-start(bf16[1,128,3584]{2,1,0:T(8,128)(2,1)} %param.11) | copy-start | bytes 2752516
  462.2 21.0 %all-to-all-start.1 = ((f32[64,1,2]{2,1,0:T(1,128)}), f32[64,1,2]{2,1,0:T(1,128)}, u32[]{:S(2)}, u32[]{:S(2)}) async-start(f32[64,1,2]{2,1,0:T(1,128)} %bitcast.3), calls=%async_computation.1 | async-start | bytes 65536 | tf_op jit(solution)/shard_map/all_to_all | solution.py:81
  497.6 19.0 %all-to-all-start.2 = ((bf16[8,64,2]{0,2,1:T(2,128)(2,1)}), bf16[8,64,2]{0,2,1:T(2,128)(2,1)S(1)}, u32[]{:S(2)}, u32[]{:S(2)}) async-start(bf16[8,64,2]{0,2,1:T(2,128)(2,1)} %copy.72), calls=%async_computation.2 | async-start | bytes 65536 | tf_op jit(solution)/shard_map/all_to_all | solution.py:57
  554.5 2.4 copy-start.4
  554.5 4.7 copy-start.1
Sparse Core Ops, SparseCore 0:
  11.1 56.5 all-gather.1
where the time goes:
time: 567 us; the launch traced here: 566 us
  waiting for transfers between devices  406 us (72%)
  local copies, waits for them, and re-layouts  70.1 us (12%)
  starting transfers between devices  27.8 us (5%)
  blocking collectives  21.6 us (4%)
  between operations  14.2 us (3%)
  matrix products  13.3 us (2%)
  other arithmetic  13.2 us (2%)
    all_to_all x1, waiting for transfers between devices, on_device(): lax.all_to_all(copies, 'node', split_axis=1, concat_axis=1, tiled=True)  324 us
    all_gather x1, waiting for transfers between devices, on_device(): lax.all_gather(departing_rows[None], 'local', axis=0, tiled=True)  56.7 us
    convert_element_type x2, local copies, waits for them, and re-layouts, on_device(): (slot_gates[:, None] * arrived_rows.astype(jnp.float32)).astype(jnp.bfloa...  22.5 us
    all_to_all x1, starting transfers between devices, on_device(): lax.all_to_all(copies, 'node', split_axis=1, concat_axis=1, tiled=True)  16 us
    reshape x1, local copies, waits for them, and re-layouts, on_device(): arrived_rows = arrived.reshape(-1, feature_count)  15.5 us
    all_gather x1, local copies, waits for them, and re-layouts, on_device(): lax.all_gather(departing_rows[None], 'local', axis=0, tiled=True)  14.7 us
    all_to_all x1, waiting for transfers between devices, on_device(): lax.all_to_all(copy_gates, 'node', split_axis=1, concat_axis=1, tiled=True)  13.6 us
    all_to_all x1, waiting for transfers between devices, on_device(): lax.all_to_all(own_terms.reshape(node_count, CAP), 'node', split_axis=0,...  11.6 us
  transfers between devices with their start and end apart: 4, of which 4 were waited for; matrix products, arithmetic and copies ran while one was open for 1% of the time, Pallas kernels for 0%

commit v1 on v0

--- a/solution.py
+++ b/solution.py
@@ -2,6 +2,7 @@
 import jax.numpy as jnp
 from jax import lax
 from jax.sharding import PartitionSpec as P
+from jax.lax import axis_index, axis_size, ppermute
 
 EXPERTS_PER_HOST = 4
 CAP = 2
@@ -42,6 +43,36 @@
 
 
 def on_device(grad_out, expert_ids, gate_weights, saved_hidden, down_weight, second_moment):
+
+    def search_types(field_in, ndim_at):
+        row_axis = "local"
+        placed = axis_size(row_axis)
+        y_new, step_out, clean = (placed, axis_index(row_axis), field_in.shape[ndim_at])
+        series = []
+        for w, b in enumerate(field_in.shape):
+            series.append(b * y_new if w == ndim_at else b)
+        b_next = lax.dynamic_update_slice_in_dim(
+            jnp.zeros(series, field_in.dtype), field_in, step_out * clean, axis=ndim_at
+        )
+        y1 = long_array = field_in
+        for u in [*range(1, y_new // 2 + 1)]:
+            ledger = []
+            for w in tuple(range(y_new)):
+                ledger.append((w, (w + 1) % y_new))
+            y1 = ppermute(y1, row_axis, ledger)
+            b_next = lax.dynamic_update_slice_in_dim(
+                b_next, y1, (step_out - u) % y_new * clean, axis=ndim_at
+            )
+            if 2 * u < y_new:
+                line_up = []
+                for w in [*range(y_new)]:
+                    line_up.append((w, (w - 1) % y_new))
+                long_array = ppermute(long_array, row_axis, line_up)
+                b_next = lax.dynamic_update_slice_in_dim(
+                    b_next, long_array, (step_out + u) % y_new * clean, axis=ndim_at
+                )
+        return b_next
+
     node_count = lax.axis_size("node")
     members = lax.axis_size("local")
     feature_count = grad_out.shape[1]
@@ -49,7 +80,7 @@
         expert_ids, gate_weights, grad_out, node_count
     )
     copies, copy_gates = (
-        lax.all_gather(departing_rows[None], "local", axis=0, tiled=True),
+        search_types(departing_rows[None], 0),
         lax.all_gather(departing_gates[None], "local", axis=0, tiled=True),
     )
     arrived, arrived_gates = (

time: 567 us -> 541 us (0.954)
  waiting for transfers between devices: 406 us -> 375 us
  between operations: 14.2 us -> 0.82 us
  starting transfers between devices: 27.8 us -> 38.8 us
  local copies, waits for them, and re-layouts: 70.1 us -> 76.5 us
    all_gather x1 -> x0, waiting for transfers between devices: 56.7 us -> none  [on_device(): lax.all_gather(departing_rows[None], 'local', axis=0, tiled=True)]
    ppermute x0 -> x7, waiting for transfers between devices: none -> 26.7 us  [the longest x4 26.7 us: search_types(): y1 = ppermute(y1, row_axis, ledger)]
    all_gather x1 -> x0, local copies, waits for them, and re-layouts: 14.7 us -> none  [on_device(): lax.all_gather(departing_rows[None], 'local', axis=0, tiled=True)]
    dynamic_update_slice x0 -> x8, local copies, waits for them, and re-layouts: none -> 13 us  [the longest x4 6.49 us: search_types(): lax.dynamic_update_slice_in_dim(b_next, y1, (step_out - u) % y_new * clea...]
    broadcast_in_dim x0 -> x1, local copies, waits for them, and re-layouts: none -> 7.57 us  [search_types(): jnp.zeros(series, field_in.dtype)]
    ppermute x0 -> x7, starting transfers between devices: none -> 6.24 us  [the longest x3 6.21 us: search_types(): long_array = ppermute(long_array, row_axis, line_up)]
  transfers between devices with their start and end apart: 4 -> 10, of which waited for: 4 -> 7; matrix products, arithmetic and copies ran while one was open for 1% -> 4% of each run, Pallas kernels for 0% -> 0%
where the time goes in v1:
time: 541 us; the launch traced here: 540 us
  waiting for transfers between devices  375 us (69%)
  local copies, waits for them, and re-layouts  76.5 us (14%)
  starting transfers between devices  38.8 us (7%)
  blocking collectives  23.8 us (4%)
  matrix products  13.6 us (3%)
  other arithmetic  12 us (2%)
    all_to_all x1, waiting for transfers between devices, on_device(): lax.all_to_all(copies, 'node', split_axis=1, concat_axis=1, tiled=True)  322 us
    ppermute x4, waiting for transfers between devices, search_types(): y1 = ppermute(y1, row_axis, ledger)  26.7 us
    convert_element_type x2, local copies, waits for them, and re-layouts, on_device(): (slot_gates[:, None] * arrived_rows.astype(jnp.float32)).astype(jnp.bfloa...  22.5 us
    all_to_all x1, starting transfers between devices, on_device(): lax.all_to_all(copies, 'node', split_axis=1, concat_axis=1, tiled=True)  18.4 us
    reshape x1, local copies, waits for them, and re-layouts, on_device(): arrived_rows = arrived.reshape(-1, feature_count)  15.5 us
    all_to_all x1, waiting for transfers between devices, on_device(): lax.all_to_all(copy_gates, 'node', split_axis=1, concat_axis=1, tiled=True)  13.8 us
    psum x1, blocking collectives, on_device(): summed = lax.psum(score_terms, 'local')  12.6 us
    all_to_all x1, waiting for transfers between devices, on_device(): lax.all_to_all(own_terms.reshape(node_count, CAP), 'node', split_axis=0,...  12.1 us
  transfers between devices with their start and end apart: 10, of which 7 were waited for; matrix products, arithmetic and copies ran while one was open for 4% of the time, Pallas kernels for 0%

profile of v1, /device:TPU:2, one launch (start us, length us, event | category | flops | bytes accessed | tf_op | source)
XLA Modules:
  0.0 540.1 jit_solution(12609895979391699327)
XLA Ops:
  0.6 0.8 fusion.23
  1.4 0.7 fusion.19
  2.3 0.2 reduce_window_sum.11
  2.4 0.2 select_reduce_fusion.2
  2.6 0.4 convolution_convert_fusion
  3.0 0.3 broadcast_in_dim_reshape.2
  3.4 1.7 collective-permute-start.1
  5.1 7.6 %broadcast_in_dim.62 = bf16[8,64,2,3584]{3,2,0,1:T(2,128)(2,1)} broadcast(bf16[]{:T(256)} %constant.92.clone.1), dimensions={} | broadcast | bytes 7340034 | tf_op jit(solution)/shard_map/broadcast_in_dim | solution.py:55
  12.7 1.6 constant_dynamic-update-slice_fusion.7
  14.3 1.9 collective-permute-done
  16.2 2.4 collective-permute-start.3
  18.6 1.6 constant_dynamic-update-slice_fusion.6
  20.3 1.7 constant_dynamic-update-slice_fusion.5
  21.9 7.8 %collective-permute-done.2 = bf16[1,64,2,3584]{3,2,0,1:T(2,128)(2,1)S(1)} collective-permute-done((bf16[1,64,2,3584]{3,2,0,1:T(2,128)(2,1)S(1)}, bf16[1,64,2,3584]{3,2,0,1:T(2,128)(2,1)S(1)}, u32[]{:S(2)}, u32[]{:S(2)}) %collective-permute-start.2) | collective-permute-done | bytes 917536 | tf_op jit(solution)/shard_map/ppermute | solution.py:62
  29.7 2.0 collective-permute-start.5
  31.8 1.6 constant_dynamic-update-slice_fusion.4
  33.4 1.6 constant_dynamic-update-slice_fusion.3
  35.0 7.5 %collective-permute-done.4 = bf16[1,64,2,3584]{3,2,0,1:T(2,128)(2,1)S(1)} collective-permute-done((bf16[1,64,2,3584]{3,2,0,1:T(2,128)(2,1)S(1)}, bf16[1,64,2,3584]{3,2,0,1:T(2,128)(2,1)S(1)}, u32[]{:S(2)}, u32[]{:S(2)}) %collective-permute-start.4) | collective-permute-done | bytes 917536 | tf_op jit(solution)/shard_map/ppermute | solution.py:62
  42.5 1.6 constant_dynamic-update-slice_fusion.2
  44.2 1.6 constant_dynamic-update-slice_fusion.1
  45.8 9.5 %collective-permute-done.6 = bf16[1,64,2,3584]{3,2,0,1:T(2,128)(2,1)S(1)} collective-permute-done((bf16[1,64,2,3584]{3,2,0,1:T(2,128)(2,1)S(1)}, bf16[1,64,2,3584]{3,2,0,1:T(2,128)(2,1)S(1)}, u32[]{:S(2)}, u32[]{:S(2)}) %collective-permute-start.6) | collective-permute-done | bytes 917536 | tf_op jit(solution)/shard_map/ppermute | solution.py:62
  55.3 1.6 constant_dynamic-update-slice_fusion
  57.0 18.4 %all-to-all-start = ((bf16[8,64,2,3584]{3,2,0,1:T(2,128)(2,1)}), bf16[8,64,2,3584]{3,2,0,1:T(2,128)(2,1)}, u32[]{:S(2)}, u32[]{:S(2)}) async-start(bf16[8,64,2,3584]{3,2,0,1:T(2,128)(2,1)} %constant_dynamic-update-slice_fusion), calls=%async_computation | async-start | bytes 14680064 | tf_op jit(solution)/shard_map/all_to_all | solution.py:87
  75.6 322.0 %all-to-all-done = bf16[8,64,2,3584]{3,2,0,1:T(2,128)(2,1)} async-done(((bf16[8,64,2,3584]{3,2,0,1:T(2,128)(2,1)}), bf16[8,64,2,3584]{3,2,0,1:T(2,128)(2,1)}, u32[]{:S(2)}, u32[]{:S(2)}) %all-to-all-start) | async-done | bytes 7340064 | tf_op jit(solution)/shard_map/all_to_all | solution.py:87
  397.5 7.4 %copy.71 = bf16[8,64,2,3584]{3,2,1,0:T(2,128)(2,1)} copy(bf16[8,64,2,3584]{3,2,0,1:T(2,128)(2,1)} %all-to-all-done) | data formatting | bytes 14680064 | tf_op jit(solution)/shard_map/all_to_all | solution.py:87
  404.9 15.5 %reshape.62 = bf16[1024,3584]{1,0:T(8,128)(2,1)} reshape(bf16[8,64,2,3584]{3,2,1,0:T(2,128)(2,1)} %copy.71) | data formatting | bytes 14680064 | tf_op jit(solution)/shard_map/reshape | solution.py:90
  420.5 5.6 %multiply_reduce_fusion = (f32[1024]{0:T(1024)S(1)}, f32[1024,128]{0,1:T(8,128)S(1)}) fusion(bf16[1,1024,128]{1,2,0:T(8,128)(2,1)S(1)} %copy.73, bf16[1024,3584]{1,0:T(8,128)(2,1)} %reshape.62, bf16[1,128,3584]{2,1,0:T(8,128)(2,1)S(1)} %copy-done.2), kind=kOutput, calls=%fused_computation.16 | convolution fusion | flops 939916288 | bytes 9048064 | tf_op jit(solution)/shard_map/dot_general | solution.py:94
  426.1 12.6 %psum.7 = f32[8,128]{1,0:T(8,128)S(1)} all-reduce(f32[8,128]{1,0:T(8,128)S(1)} %bitcast.47), channel_id=1, replica_groups=mesh['node'=64,'local'=8] {'local'}, use_global_device_ids=true, to_apply=%region_5.6 | all-reduce | flops 1024 | bytes 8192 | tf_op jit(solution)/shard_map/psum | solution.py:110
  438.7 0.8 all_to_all.13
  439.5 9.5 %all-to-all-start.1 = ((f32[64,1,2]{2,1,0:T(1,128)}), f32[64,1,2]{2,1,0:T(1,128)}, u32[]{:S(2)}, u32[]{:S(2)}) async-start(f32[64,1,2]{2,1,0:T(1,128)} %bitcast.6), calls=%async_computation.1 | async-start | bytes 65536 | tf_op jit(solution)/shard_map/all_to_all | solution.py:112
  449.1 0.6 copy.72
  449.7 1.3 copy.82
  451.0 12.1 %all-to-all-done.1 = f32[64,1,2]{2,1,0:T(1,128)} async-done(((f32[64,1,2]{2,1,0:T(1,128)}), f32[64,1,2]{2,1,0:T(1,128)}, u32[]{:S(2)}, u32[]{:S(2)}) %all-to-all-start.1) | async-done | bytes 544 | tf_op jit(solution)/shard_map/all_to_all | solution.py:112
  463.1 0.5 broadcast.54
  463.6 1.5 reduce.7
  465.6 11.2 %all_gather.3 = bf16[8,64,2]{1,2,0:T(2,128)(2,1)S(1)} all-gather(bf16[1,64,2]{1,2,0:T(2,128)(2,1)S(1)} %copy.75), channel_id=1, replica_groups=mesh['node'=64,'local'=8] {'local'}, dimensions={0}, use_global_device_ids=true | all-gather | bytes 2304 | tf_op jit(solution)/shard_map/all_gather | solution.py:84
  476.8 0.7 copy.76
  477.6 4.6 all-to-all-start.2
  482.2 0.6 broadcast_select_fusion
  482.8 13.8 %all-to-all-done.2 = bf16[8,64,2]{0,2,1:T(2,128)(2,1)S(1)} async-done(((bf16[8,64,2]{0,2,1:T(2,128)(2,1)}), bf16[8,64,2]{0,2,1:T(2,128)(2,1)S(1)}, u32[]{:S(2)}, u32[]{:S(2)}) %all-to-all-start.2) | async-done | bytes 2080 | tf_op jit(solution)/shard_map/all_to_all | solution.py:88
  496.8 7.8 %multiply_convert_fusion = bf16[8,64,2,3584]{3,1,2,0:T(8,128)(2,1)S(1)} fusion(bf16[8,64,2,3584]{3,2,0,1:T(2,128)(2,1)} %all-to-all-done, f32[8,64,2]{1,2,0:T(2,128)S(1)} %copy.79), kind=kLoop, calls=%fused_computation | loop fusion | flops 11010048 | bytes 14684160 | tf_op jit(solution)/shard_map/convert_element_type | solution.py:99
  504.6 7.1 %copy.81 = bf16[8,64,2,3584]{3,2,1,0:T(2,128)(2,1)} copy(bf16[8,64,2,3584]{3,1,2,0:T(8,128)(2,1)S(1)} %multiply_convert_fusion) | data formatting | bytes 14680064 | tf_op jit(solution)/shard_map/convert_element_type | solution.py:99
  511.6 15.4 %convert_element_type.90 = bf16[1024,3584]{1,0:T(8,128)(2,1)} reshape(bf16[8,64,2,3584]{3,2,1,0:T(2,128)(2,1)} %copy.81) | data formatting | bytes 14680064 | tf_op jit(solution)/shard_map/convert_element_type | solution.py:99
  527.1 7.6 %fusion.5 = (bf16[1,128,3584]{1,2,0:T(8,128)(2,1)}, bf16[1,128,3584]{1,2,0:T(8,128)(2,1)}) fusion(bf16[1,128,3584]{1,2,0:T(8,128)(2,1)} %copy.82, bf16[1,128,3584]{1,2,0:T(8,128)(2,1)S(1)} %copy.72, bf16[1024,3584]{1,0:T(8,128)(2,1)} %convert_element_type.90, bf16[1,1024,128]{2,1,0:T(8,128)(2,1)S(1)} %copy-done.4), kind=kOutput, calls=%fused_computation.11 | convolution fusion | flops 946405376 | bytes 11272192 | tf_op jit(solution)/shard_map/dot_general | solution.py:100
  534.6 2.2 copy.84
  536.9 2.2 copy.85
  539.1 0.2 reshape.64
  539.3 0.8 copy.83
  (33 shorter events, 1.2 us)
Async XLA Ops:
  0.6 2.0 copy-start
  3.4 12.8 %collective-permute-start = (bf16[1,64,2,3584]{3,2,0,1:T(2,128)(2,1)S(1)}, bf16[1,64,2,3584]{3,2,0,1:T(2,128)(2,1)S(1)}, u32[]{:S(2)}, u32[]{:S(2)}) collective-permute-start(bf16[1,64,2,3584]{3,2,0,1:T(2,128)(2,1)S(1)} %bitcast.45), channel_id=1, source_target_pairs={{0,1},{1,2},{2,3},{3,4},{4,5},{5,6},{6,7},{7,0},{8,9},{9,10},{10,1... | collective-permute-start | bytes 2752520 | tf_op jit(solution)/shard_map/ppermute | solution.py:62
  3.4 12.8 %collective-permute-start.1 = (bf16[1,64,2,3584]{3,2,0,1:T(2,128)(2,1)S(1)}, bf16[1,64,2,3584]{3,2,0,1:T(2,128)(2,1)S(1)}, u32[]{:S(2)}, u32[]{:S(2)}) collective-permute-start(bf16[1,64,2,3584]{3,2,0,1:T(2,128)(2,1)S(1)} %bitcast.46), channel_id=1, source_target_pairs={{0,7},{1,0},{2,1},{3,2},{4,3},{5,4},{6,5},{7,6},{8,15},{9,8},{10,9... | collective-permute-start | bytes 2752520 | tf_op jit(solution)/shard_map/ppermute | solution.py:70
  16.2 13.5 %collective-permute-start.2 = (bf16[1,64,2,3584]{3,2,0,1:T(2,128)(2,1)S(1)}, bf16[1,64,2,3584]{3,2,0,1:T(2,128)(2,1)S(1)}, u32[]{:S(2)}, u32[]{:S(2)}) collective-permute-start(bf16[1,64,2,3584]{3,2,0,1:T(2,128)(2,1)S(1)} %collective-permute-done), channel_id=1, source_target_pairs={{0,1},{1,2},{2,3},{3,4},{4,5},{5,6},{6,7},{7,0},{8,9},{9,10},{10,1... | collective-permute-start | bytes 2752520 | tf_op jit(solution)/shard_map/ppermute | solution.py:62
  16.2 13.5 %collective-permute-start.3 = (bf16[1,64,2,3584]{3,2,0,1:T(2,128)(2,1)S(1)}, bf16[1,64,2,3584]{3,2,0,1:T(2,128)(2,1)S(1)}, u32[]{:S(2)}, u32[]{:S(2)}) collective-permute-start(bf16[1,64,2,3584]{3,2,0,1:T(2,128)(2,1)S(1)} %collective-permute-done.1), channel_id=1, source_target_pairs={{0,7},{1,0},{2,1},{3,2},{4,3},{5,4},{6,5},{7,6},{8,15},{9,8},{10,9... | collective-permute-start | bytes 2752520 | tf_op jit(solution)/shard_map/ppermute | solution.py:70
  29.7 12.8 %collective-permute-start.4 = (bf16[1,64,2,3584]{3,2,0,1:T(2,128)(2,1)S(1)}, bf16[1,64,2,3584]{3,2,0,1:T(2,128)(2,1)S(1)}, u32[]{:S(2)}, u32[]{:S(2)}) collective-permute-start(bf16[1,64,2,3584]{3,2,0,1:T(2,128)(2,1)S(1)} %collective-permute-done.2), channel_id=1, source_target_pairs={{0,1},{1,2},{2,3},{3,4},{4,5},{5,6},{6,7},{7,0},{8,9},{9,10},{10,1... | collective-permute-start | bytes 2752520 | tf_op jit(solution)/shard_map/ppermute | solution.py:62
  29.7 14.4 %collective-permute-start.5 = (bf16[1,64,2,3584]{3,2,0,1:T(2,128)(2,1)S(1)}, bf16[1,64,2,3584]{3,2,0,1:T(2,128)(2,1)S(1)}, u32[]{:S(2)}, u32[]{:S(2)}) collective-permute-start(bf16[1,64,2,3584]{3,2,0,1:T(2,128)(2,1)S(1)} %collective-permute-done.3), channel_id=1, source_target_pairs={{0,7},{1,0},{2,1},{3,2},{4,3},{5,4},{6,5},{7,6},{8,15},{9,8},{10,9... | collective-permute-start | bytes 2752520 | tf_op jit(solution)/shard_map/ppermute | solution.py:70
  42.5 12.8 %collective-permute-start.6 = (bf16[1,64,2,3584]{3,2,0,1:T(2,128)(2,1)S(1)}, bf16[1,64,2,3584]{3,2,0,1:T(2,128)(2,1)S(1)}, u32[]{:S(2)}, u32[]{:S(2)}) collective-permute-start(bf16[1,64,2,3584]{3,2,0,1:T(2,128)(2,1)S(1)} %collective-permute-done.4), channel_id=1, source_target_pairs={{0,1},{1,2},{2,3},{3,4},{4,5},{5,6},{6,7},{7,0},{8,9},{9,10},{10,1... | collective-permute-start | bytes 2752520 | tf_op jit(solution)/shard_map/ppermute | solution.py:62
  57.0 18.4 %copy-start.4 = (bf16[1,1024,128]{2,1,0:T(8,128)(2,1)S(1)}, bf16[1,1024,128]{2,1,0:T(8,128)(2,1)}, u32[]{:S(2)}) copy-start(bf16[1,1024,128]{2,1,0:T(8,128)(2,1)} %param.9) | copy-start | bytes 786436
  57.0 340.5 %all-to-all-start = ((bf16[8,64,2,3584]{3,2,0,1:T(2,128)(2,1)}), bf16[8,64,2,3584]{3,2,0,1:T(2,128)(2,1)}, u32[]{:S(2)}, u32[]{:S(2)}) async-start(bf16[8,64,2,3584]{3,2,0,1:T(2,128)(2,1)} %constant_dynamic-update-slice_fusion), calls=%async_computation | async-start | bytes 14680064 | tf_op jit(solution)/shard_map/all_to_all | solution.py:87
  404.9 15.5 %copy-start.2 = (bf16[1,128,3584]{2,1,0:T(8,128)(2,1)S(1)}, bf16[1,128,3584]{2,1,0:T(8,128)(2,1)}, u32[]{:S(2)}) copy-start(bf16[1,128,3584]{2,1,0:T(8,128)(2,1)} %param.10) | copy-start | bytes 2752516
  420.5 28.5 %copy-start.5 = (f32[128,8]{0,1:T(8,128)S(1)}, f32[128,8]{0,1:T(8,128)}, u32[]{:S(2)}) copy-start(f32[128,8]{0,1:T(8,128)} %param.8) | copy-start | bytes 12292
  420.5 29.2 %copy-start.3 = (bf16[1,128,3584]{2,1,0:T(8,128)(2,1)S(1)}, bf16[1,128,3584]{2,1,0:T(8,128)(2,1)}, u32[]{:S(2)}) copy-start(bf16[1,128,3584]{2,1,0:T(8,128)(2,1)} %param.11) | copy-start | bytes 2752516
  439.5 23.6 %all-to-all-start.1 = ((f32[64,1,2]{2,1,0:T(1,128)}), f32[64,1,2]{2,1,0:T(1,128)}, u32[]{:S(2)}, u32[]{:S(2)}) async-start(f32[64,1,2]{2,1,0:T(1,128)} %bitcast.6), calls=%async_computation.1 | async-start | bytes 65536 | tf_op jit(solution)/shard_map/all_to_all | solution.py:112
  477.6 19.0 %all-to-all-start.2 = ((bf16[8,64,2]{0,2,1:T(2,128)(2,1)}), bf16[8,64,2]{0,2,1:T(2,128)(2,1)S(1)}, u32[]{:S(2)}, u32[]{:S(2)}) async-start(bf16[8,64,2]{0,2,1:T(2,128)(2,1)} %copy.76), calls=%async_computation.2 | async-start | bytes 65536 | tf_op jit(solution)/shard_map/all_to_all | solution.py:88
  527.1 13.1 %copy-start.1 = (bf16[128,3584]{1,0:T(8,128)(2,1)S(1)}, bf16[128,3584]{1,0:T(8,128)(2,1)}, u32[]{:S(2)}) copy-start(bf16[128,3584]{1,0:T(8,128)(2,1)} %param.6) | copy-start | bytes 2752516
